TPU v7x, 256 devices: a whole 4x4x8 slice. The times are simulated.
256 devices in a mesh: fx: 32 (over z, y), fy: 4 (over x), fz: 2 (over core).
Axes of the slice: x: 4, y: 4, z: 8, core: 2. Of those that a mesh axis runs over, the one named last changes fastest.
Arguments:
- state: float32 [5, 16, 1024, 512], P(None, 'fz', 'fx', 'fy'), may hold values from -6 to 6
- kappa: float32 [16, 1024, 512], P('fz', 'fx', 'fy'), may hold values from 0.25 to 1
- mix: float32 [5, 5], replicated, may hold values from -0.16 to 0.16
- press_weight: float32 [5], replicated, may hold values from 0.5 to 1.5
- source_weight: float32 [5], replicated, may hold values from 0.05 to 0.2
- interp: float32 [128, 128], replicated, may hold values from -0.25 to 0.25
- block_inverse: float32 [512, 128, 128], P('fx'), as said below
- coupling: float32 [512, 128, 128], P('fx'), may hold values from -0.125 to 0.125
- front_order: int32 [32, 16], P('fx'), may hold values from 0 to 15, each once within a row
- face_owner: int32 [4096, 1], P(('fx', 'fy')), may hold values from 0 to 31; in each aligned block of 32 rows (0 to 31, 32 to 63, ...) at most 2 rows name the same one
- face_slot: int32 [4096], P(('fx', 'fy')), may hold values from 0 to 15
Outputs:
- state_out: float32 [5, 16, 1024, 512], P(None, 'fz', 'fx', 'fy')
- displacement: float32 [512, 128], P('fx')
Inputs may be any that keep to these rules, and one draw needn't show every extreme that they name: `face_owner`: in the rows of one device no owner is named more than 2 times; every draw has some device naming one owner exactly 2 times. `front_order`: each row lists every block of one owner once. `block_inverse`: each block is the inverse of a stiffness block.
All inputs are finite; a program needn't handle non-finite values.
Results may differ from a plain program's by a relative error of at most 0.00021.
Values sent between devices are 32-bit elements; how exact they have to be, the bound alone decides.
A program may use at most 64 MiB of HBM per device.

v0:
```python
import jax
import jax.numpy as jnp
from jax import lax
from jax.sharding import PartitionSpec as P

ITERS = 3
DIFFUSION = 0.16
HIGHEST = lax.Precision.HIGHEST


def with_halo(cells, sides, width):
    for axis, dim in sides:
        count = lax.axis_size(axis)
        ends = count - 1
        head = lax.slice_in_dim(cells, 0, width, axis=dim)
        tail = lax.slice_in_dim(cells, cells.shape[dim] - width, cells.shape[dim], axis=dim)
        cells = jnp.concatenate(
            [
                lax.ppermute(tail, axis, [(i, (i + 1) % count) for i in range(ends)]),
                cells,
                lax.ppermute(head, axis, [((i + 1) % count, i) for i in range(ends)]),
            ],
            axis=dim,
        )
    return cells


def sweep_core(padded, coeff, mix):
    centre = padded[:, 1:-1, 1:-1, 1:-1]
    beside = padded[:, 2:, 1:-1, 1:-1] + padded[:, :-2, 1:-1, 1:-1]
    beside = beside + padded[:, 1:-1, 2:, 1:-1] + padded[:, 1:-1, :-2, 1:-1]
    beside = beside + padded[:, 1:-1, 1:-1, 2:] + padded[:, 1:-1, 1:-1, :-2]
    mixed = jnp.einsum("cd,dzxy->czxy", mix, centre, precision=HIGHEST)
    return centre + DIFFUSION * coeff[None] * (beside - 6.0 * centre) + mixed


def frontal(block_loads, inverse, coupling, order):
    blocks_owner, block_dofs = block_loads.shape

    def advance(position, carry):
        previous, solved = carry
        target = order[position]
        right_side = block_loads[target] - jnp.dot(coupling[target], previous, precision=HIGHEST)
        current = jnp.dot(inverse[target], right_side, precision=HIGHEST)
        return (current, solved.at[target].set(current))

    start = (
        jnp.zeros((block_dofs,), jnp.float32),
        jnp.zeros((blocks_owner, block_dofs), jnp.float32),
    )
    return lax.fori_loop(0, blocks_owner, advance, start)[1]


def on_device(
    state,
    kappa,
    mix,
    press_weight,
    source_weight,
    interp,
    block_inverse,
    coupling,
    front_order,
    face_owner,
    face_slot,
):
    count_z, count_x, count_y = kappa.shape
    blocks_owner = block_inverse.shape[0]
    owners = lax.axis_size("fx")
    wall_mask = (lax.axis_index("fz") == 0).astype(jnp.float32)
    total_z = count_z * lax.axis_size("fz")
    heights = (lax.axis_index("fz") * count_z + jnp.arange(count_z)).astype(jnp.float32)
    profile = 1.0 - heights / total_z
    owner_of = face_owner[:, 0]
    spread = (
        jnp.arange(owners * blocks_owner)[:, None] == (owner_of * blocks_owner + face_slot)[None, :]
    ).astype(jnp.float32)
    displacement = jnp.zeros((blocks_owner, interp.shape[1]), jnp.float32)
    for iteration in range(ITERS):
        for sweep_index in range(2):
            padded = with_halo(state, (("fx", 2), ("fy", 3), ("fz", 1)), 1)
            state = sweep_core(padded, kappa, mix)
        pressure = jnp.sum(press_weight[:, None, None] * state[:, 0], axis=0) * wall_mask
        outgoing = jnp.dot(spread, pressure, precision=HIGHEST)
        incoming = lax.all_to_all(outgoing, "fx", split_axis=0, concat_axis=0, tiled=True)
        forces = jnp.sum(incoming.reshape(owners, blocks_owner, count_y), axis=0)
        forces = lax.psum(forces, ("fy", "fz"))
        block_loads = jnp.dot(forces, interp, precision=HIGHEST)
        displacement = frontal(block_loads, block_inverse, coupling, front_order[0])
        face_disp = jnp.dot(displacement, interp.T, precision=HIGHEST)
        every_block = lax.all_gather(face_disp, "fx", axis=0, tiled=True)
        wall_disp = jnp.dot(spread.T, every_block, precision=HIGHEST)
        state = (
            state
            + source_weight[:, None, None, None]
            * profile[None, :, None, None]
            * wall_disp[None, None]
        )
    return (state, displacement)


def solution(mesh):
    return jax.shard_map(
        on_device,
        mesh=mesh,
        in_specs=(
            P(None, "fz", "fx", "fy"),
            P("fz", "fx", "fy"),
            P(),
            P(),
            P(),
            P(),
            P("fx", None, None),
            P("fx", None, None),
            P("fx", None),
            P(("fx", "fy"), None),
            P(("fx", "fy")),
        ),
        out_specs=(P(None, "fz", "fx", "fy"), P("fx", None)),
        check_vma=False,
    )
```

profile of v0, /device:TPU:8, one launch (start us, length us, event | category | flops | bytes accessed | tf_op | source)
XLA Modules:
  0.0 744.5 jit_solution(12291830759761344540)
XLA Ops:
  2.2 3.5 collective-permute-start
  14.6 3.4 collective-permute-start.2
  20.3 3.8 collective-permute-done.3
  40.5 4.8 collective-permute-done.7
  46.8 3.4 collective-permute-start.8
  52.5 3.9 collective-permute-done.9
  60.0 4.5 collective-permute-start.11
  65.3 4.5 fusion.37
  71.9 13.9 %all-to-all-start = ((f32[32,16,128]{2,1,0:T(8,128)}), f32[32,16,128]{2,1,0:T(8,128)S(1)}, u32[]{:S(2)}, u32[]{:S(2)}) async-start(f32[32,16,128]{2,1,0:T(8,128)} %bitcast.34), calls=%async_computation | async-start | bytes 524288 | tf_op jit(solution)/shard_map/all_to_all | solution.py:85
  86.6 10.9 %all-to-all-done = f32[32,16,128]{2,1,0:T(8,128)S(1)} async-done(((f32[32,16,128]{2,1,0:T(8,128)}), f32[32,16,128]{2,1,0:T(8,128)S(1)}, u32[]{:S(2)}, u32[]{:S(2)}) %all-to-all-start) | async-done | bytes 262176 | tf_op jit(solution)/shard_map/all_to_all | solution.py:85
  97.5 12.7 %psum.21 = f32[16,128]{1,0:T(8,128)S(1)} all-reduce(f32[16,128]{1,0:T(8,128)S(1)} %reduce_sum.55), channel_id=1, replica_groups=mesh['fx'=32,'fy'=4,'fz'=2] {'fy','fz'}, use_global_device_ids=true, to_apply=%region_2.0 | all-reduce | flops 2048 | bytes 16384 | tf_op jit(solution)/shard_map/psum | solution.py:87
  110.4 97.6 %while.48 = (s32[]{:T(128)}, f32[128]{0:T(128)S(1)}, f32[16,128]{1,0:T(8,128)S(1)}, s32[16]{0:T(128)S(1)}, f32[16,128,128]{2,1,0:T(8,128)}, /*index=5*/f32[16,12...) while((s32[]{:T(128)}, f32[128]{0:T(128)S(1)}, ...), condition=%wide.region_5.0_spmd, body=%wide.region_3.0_spmd.sunk | while | flops 393486 | bytes 138424 | solution.py:51
  208.2 48.1 %all_gather.9 = f32[512,128]{1,0:T(8,128)S(1)} all-gather(f32[16,128]{1,0:T(8,128)S(1)} %fusion.129), channel_id=1, replica_groups=mesh['fx'=32,'fy'=4,'fz'=2] {'fx'}, dimensions={0}, use_global_device_ids=true | all-gather | bytes 270336 | tf_op jit(solution)/shard_map/all_gather | solution.py:91
  259.3 3.3 collective-permute-start.13
  270.2 3.8 collective-permute-done.15
  284.5 3.9 collective-permute-start.18
  290.4 5.4 collective-permute-done.19
  302.9 3.8 collective-permute-done.21
  319.3 10.7 %all-to-all-start.1 = ((f32[32,16,128]{2,1,0:T(8,128)}), f32[32,16,128]{2,1,0:T(8,128)S(1)}, u32[]{:S(2)}, u32[]{:S(2)}) async-start(f32[32,16,128]{2,1,0:T(8,128)} %bitcast.38), calls=%async_computation.1 | async-start | bytes 524288 | tf_op jit(solution)/shard_map/all_to_all | solution.py:85
  329.9 11.7 %all-to-all-done.1 = f32[32,16,128]{2,1,0:T(8,128)S(1)} async-done(((f32[32,16,128]{2,1,0:T(8,128)}), f32[32,16,128]{2,1,0:T(8,128)S(1)}, u32[]{:S(2)}, u32[]{:S(2)}) %all-to-all-start.1) | async-done | bytes 262176 | tf_op jit(solution)/shard_map/all_to_all | solution.py:85
  341.7 12.7 %psum.22 = f32[16,128]{1,0:T(8,128)S(1)} all-reduce(f32[16,128]{1,0:T(8,128)S(1)} %reduce_sum.57), channel_id=1, replica_groups=mesh['fx'=32,'fy'=4,'fz'=2] {'fy','fz'}, use_global_device_ids=true, to_apply=%region_8.0 | all-reduce | flops 2048 | bytes 16384 | tf_op jit(solution)/shard_map/psum | solution.py:87
  354.6 97.6 %while.49 = (s32[]{:T(128)}, f32[128]{0:T(128)S(1)}, f32[16,128]{1,0:T(8,128)S(1)}, s32[16]{0:T(128)S(1)}, f32[16,128,128]{2,1,0:T(8,128)}, /*index=5*/f32[16,12...) while((s32[]{:T(128)}, f32[128]{0:T(128)S(1)}, ...), condition=%wide.region_11.0_spmd, body=%wide.region_9.0_spmd.sunk | while | flops 393486 | bytes 138424 | solution.py:51
  452.3 48.1 %all_gather.10 = f32[512,128]{1,0:T(8,128)S(1)} all-gather(f32[16,128]{1,0:T(8,128)S(1)} %fusion.131), channel_id=1, replica_groups=mesh['fx'=32,'fy'=4,'fz'=2] {'fx'}, dimensions={0}, use_global_device_ids=true | all-gather | bytes 270336 | tf_op jit(solution)/shard_map/all_gather | solution.py:91
  514.5 3.8 collective-permute-done.27
  528.7 3.9 collective-permute-start.30
  534.6 5.4 collective-permute-done.31
  547.1 3.8 collective-permute-done.33
  562.4 10.8 %all-to-all-start.2 = ((f32[32,16,128]{2,1,0:T(8,128)}), f32[32,16,128]{2,1,0:T(8,128)S(1)}, u32[]{:S(2)}, u32[]{:S(2)}) async-start(f32[32,16,128]{2,1,0:T(8,128)} %bitcast.42), calls=%async_computation.2 | async-start | bytes 524288 | tf_op jit(solution)/shard_map/all_to_all | solution.py:85
  573.2 11.7 %all-to-all-done.2 = f32[32,16,128]{2,1,0:T(8,128)S(1)} async-done(((f32[32,16,128]{2,1,0:T(8,128)}), f32[32,16,128]{2,1,0:T(8,128)S(1)}, u32[]{:S(2)}, u32[]{:S(2)}) %all-to-all-start.2) | async-done | bytes 262176 | tf_op jit(solution)/shard_map/all_to_all | solution.py:85
  585.0 12.7 %psum.23 = f32[16,128]{1,0:T(8,128)S(1)} all-reduce(f32[16,128]{1,0:T(8,128)S(1)} %reduce_sum.59), channel_id=1, replica_groups=mesh['fx'=32,'fy'=4,'fz'=2] {'fy','fz'}, use_global_device_ids=true, to_apply=%region_14.0 | all-reduce | flops 2048 | bytes 16384 | tf_op jit(solution)/shard_map/psum | solution.py:87
  597.9 97.0 %while.50 = (s32[]{:T(128)}, f32[128]{0:T(128)S(1)}, f32[16,128]{1,0:T(8,128)S(1)}, s32[16]{0:T(128)S(1)}, f32[16,128,128]{2,1,0:T(8,128)}, /*index=5*/f32[16,12...) while((s32[]{:T(128)}, f32[128]{0:T(128)S(1)}, ...), condition=%wide.region_17.0_spmd, body=%wide.region_15.0_spmd.sunk | while | flops 393486 | bytes 138424 | solution.py:51
  695.1 47.9 %all_gather.11 = f32[512,128]{1,0:T(8,128)S(1)} all-gather(f32[16,128]{1,0:T(8,128)S(1)} %fusion.133), channel_id=1, replica_groups=mesh['fx'=32,'fy'=4,'fz'=2] {'fx'}, dimensions={0}, use_global_device_ids=true | all-gather | bytes 270336 | tf_op jit(solution)/shard_map/all_gather | solution.py:91
  (440 shorter events, 327.8 us)
Async XLA Ops:
  2.2 5.9 collective-permute-start
  5.7 5.8 collective-permute-start.1
  14.6 5.1 collective-permute-start.2
  18.4 5.7 collective-permute-start.3
  27.1 4.4 collective-permute-start.4
  28.4 4.2 collective-permute-start.5
  34.6 5.9 collective-permute-start.6
  37.8 7.5 %collective-permute-start.7 = (f32[5,8,1,128]{3,0,2,1:T(8,128)S(1)}, f32[5,8,1,128]{3,0,2,1:T(8,128)S(1)}, u32[]{:S(2)}, u32[]{:S(2)}) collective-permute-start(f32[5,8,1,128]{3,0,2,1:T(8,128)S(1)} %get-tuple-element.528), channel_id=1, source_target_pairs={{8,0},{16,8},{24,16},{32,24},{40,32},{48,40},{56,48},{64,56},{72,6... | collective-permute-start | bytes 61448 | tf_op jit(solution)/shard_map/ppermute | solution.py:21
  46.8 5.1 collective-permute-start.8
  50.6 5.8 collective-permute-start.9
  58.8 5.8 collective-permute-start.10
  60.0 5.2 collective-permute-start.11
  71.9 25.6 %all-to-all-start = ((f32[32,16,128]{2,1,0:T(8,128)}), f32[32,16,128]{2,1,0:T(8,128)S(1)}, u32[]{:S(2)}, u32[]{:S(2)}) async-start(f32[32,16,128]{2,1,0:T(8,128)} %bitcast.34), calls=%async_computation | async-start | bytes 524288 | tf_op jit(solution)/shard_map/all_to_all | solution.py:85
  256.8 5.9 collective-permute-start.12
  259.3 5.8 collective-permute-start.13
  268.4 5.7 collective-permute-start.15
  277.0 4.4 collective-permute-start.16
  278.3 4.2 collective-permute-start.17
  284.5 5.9 collective-permute-start.18
  288.5 7.4 collective-permute-start.19
  301.0 5.7 collective-permute-start.21
  309.7 4.4 collective-permute-start.22
  319.3 22.4 %all-to-all-start.1 = ((f32[32,16,128]{2,1,0:T(8,128)}), f32[32,16,128]{2,1,0:T(8,128)S(1)}, u32[]{:S(2)}, u32[]{:S(2)}) async-start(f32[32,16,128]{2,1,0:T(8,128)} %bitcast.38), calls=%async_computation.1 | async-start | bytes 524288 | tf_op jit(solution)/shard_map/all_to_all | solution.py:85
  501.0 5.9 collective-permute-start.24
  503.5 5.8 collective-permute-start.25
  512.6 5.7 collective-permute-start.27
  521.2 4.4 collective-permute-start.28
  528.7 5.9 collective-permute-start.30
  532.7 7.4 collective-permute-start.31
  545.2 5.7 collective-permute-start.33
  553.9 4.4 collective-permute-start.34
  562.4 22.5 %all-to-all-start.2 = ((f32[32,16,128]{2,1,0:T(8,128)}), f32[32,16,128]{2,1,0:T(8,128)S(1)}, u32[]{:S(2)}, u32[]{:S(2)}) async-start(f32[32,16,128]{2,1,0:T(8,128)} %bitcast.42), calls=%async_computation.2 | async-start | bytes 524288 | tf_op jit(solution)/shard_map/all_to_all | solution.py:85
  (35 other events, 846.3 us)
where the time goes:
time: 752 us; the launch traced here: 744 us
  blocking collectives  182 us (24%)
  matrix products  149 us (20%)
  starting transfers between devices  118 us (16%)
  loops' own time  94.4 us (13%)
  waiting for transfers between devices  87.3 us (12%)
  local copies, waits for them, and re-layouts  64.7 us (9%)
  other arithmetic  46.7 us (6%)
    all_gather x3, blocking collectives, on_device(): every_block = lax.all_gather(face_disp, 'fx', axis=0, tiled=True)  144 us
    another operation x3, loops' own time, frontal(): return lax.fori_loop(0, blocks_owner, advance, start)[1]  94.4 us
    dot_general x48, matrix products, advance(): current = jnp.dot(inverse[target], right_side, precision=HIGHEST)  81.6 us
    ppermute x18, starting transfers between devices, with_halo(): lax.ppermute(tail, axis, [(i, (i + 1) % count) for i in range(ends)])  51.9 us
    dot_general x48, matrix products, advance(): jnp.dot(coupling[target], previous, precision=HIGHEST)  48.8 us
    ppermute x18, waiting for transfers between devices, with_halo(): lax.ppermute(head, axis, [((i + 1) % count, i) for i in range(ends)])  46.5 us
    psum x3, blocking collectives, on_device(): forces = lax.psum(forces, ('fy', 'fz'))  38 us
    another operation x48, other arithmetic  36.6 us
  transfers between devices with their start and end apart: 39, of which 21 were waited for; matrix products, arithmetic and copies ran while one was open for 1% of the time, Pallas kernels for 0%

commit v1 on v0

--- a/solution.py
+++ b/solution.py
@@ -88,7 +88,9 @@
         block_loads = jnp.dot(forces, interp, precision=HIGHEST)
         displacement = frontal(block_loads, block_inverse, coupling, front_order[0])
         face_disp = jnp.dot(displacement, interp.T, precision=HIGHEST)
-        every_block = lax.all_gather(face_disp, "fx", axis=0, tiled=True)
+        every_block = jnp.concatenate(
+            lax.all_to_all(jnp.stack([face_disp] * lax.axis_size("fx")), "fx", 0, 0), axis=0
+        )
         wall_disp = jnp.dot(spread.T, every_block, precision=HIGHEST)
         state = (
             state

time: 752 us -> 660 us (0.88)
  blocking collectives: 182 us -> 71.1 us
  waiting for transfers between devices: 87.3 us -> 101 us
    all_gather x3 -> x0, blocking collectives: 144 us -> none  [on_device(): every_block = lax.all_gather(face_disp, 'fx', axis=0, tiled=True)]
    all_to_all x0 -> x2, blocking collectives: none -> 33.1 us  [on_device(): lax.all_to_all(jnp.stack([face_disp] * lax.axis_size('fx')), 'fx', 0, 0)]
    all_to_all x0 -> x1, waiting for transfers between devices: none -> 11.5 us  [on_device(): lax.all_to_all(jnp.stack([face_disp] * lax.axis_size('fx')), 'fx', 0, 0)]
  transfers between devices with their start and end apart: 39 -> 40, of which waited for: 21 -> 22; matrix products, arithmetic and copies ran while one was open for 1% -> 1% of each run, Pallas kernels for 0% -> 0%
where the time goes in v1:
time: 660 us; the launch traced here: 651 us
  matrix products  150 us (23%)
  starting transfers between devices  121 us (18%)
  waiting for transfers between devices  101 us (15%)
  loops' own time  94.4 us (14%)
  blocking collectives  71.1 us (11%)
  local copies, waits for them, and re-layouts  65.4 us (10%)
  other arithmetic  45.9 us (7%)
    another operation x3, loops' own time, frontal(): return lax.fori_loop(0, blocks_owner, advance, start)[1]  94.4 us
    dot_general x48, matrix products, advance(): current = jnp.dot(inverse[target], right_side, precision=HIGHEST)  82 us
    ppermute x18, starting transfers between devices, with_halo(): lax.ppermute(tail, axis, [(i, (i + 1) % count) for i in range(ends)])  53.6 us
    dot_general x48, matrix products, advance(): jnp.dot(coupling[target], previous, precision=HIGHEST)  48.8 us
    ppermute x18, waiting for transfers between devices, with_halo(): lax.ppermute(head, axis, [((i + 1) % count, i) for i in range(ends)])  48.2 us
    psum x3, blocking collectives, on_device(): forces = lax.psum(forces, ('fy', 'fz'))  38 us
    another operation x48, other arithmetic  36.5 us
    all_to_all x3, waiting for transfers between devices, on_device(): lax.all_to_all(outgoing, 'fx', split_axis=0, concat_axis=0, tiled=True)  35.2 us
  transfers between devices with their start and end apart: 40, of which 22 were waited for; matrix products, arithmetic and copies ran while one was open for 1% of the time, Pallas kernels for 0%

profile of v1, /device:TPU:8, one launch (start us, length us, event | category | flops | bytes accessed | tf_op | source)
XLA Modules:
  0.0 651.2 jit_solution(16397881675791273280)
XLA Ops:
  2.2 3.5 collective-permute-start
  14.6 3.4 collective-permute-start.2
  20.3 3.8 collective-permute-done.3
  40.4 4.8 collective-permute-done.7
  46.7 3.4 collective-permute-start.8
  52.4 3.9 collective-permute-done.9
  60.0 4.5 collective-permute-start.11
  65.3 4.5 fusion.37
  71.8 13.9 %all-to-all-start = ((f32[32,16,128]{2,1,0:T(8,128)}), f32[32,16,128]{2,1,0:T(8,128)S(1)}, u32[]{:S(2)}, u32[]{:S(2)}) async-start(f32[32,16,128]{2,1,0:T(8,128)} %bitcast.34), calls=%async_computation | async-start | bytes 524288 | tf_op jit(solution)/shard_map/all_to_all | solution.py:85
  85.7 11.7 %all-to-all-done = f32[32,16,128]{2,1,0:T(8,128)S(1)} async-done(((f32[32,16,128]{2,1,0:T(8,128)}), f32[32,16,128]{2,1,0:T(8,128)S(1)}, u32[]{:S(2)}, u32[]{:S(2)}) %all-to-all-start) | async-done | bytes 262176 | tf_op jit(solution)/shard_map/all_to_all | solution.py:85
  97.5 12.7 %psum.21 = f32[16,128]{1,0:T(8,128)S(1)} all-reduce(f32[16,128]{1,0:T(8,128)S(1)} %reduce_sum.55), channel_id=1, replica_groups=mesh['fx'=32,'fy'=4,'fz'=2] {'fy','fz'}, use_global_device_ids=true, to_apply=%region_2.0 | all-reduce | flops 2048 | bytes 16384 | tf_op jit(solution)/shard_map/psum | solution.py:87
  110.4 98.6 %while.48 = (s32[]{:T(128)}, f32[128]{0:T(128)S(1)}, f32[16,128]{1,0:T(8,128)S(1)}, s32[16]{0:T(128)S(1)}, f32[16,128,128]{2,1,0:T(8,128)}, /*index=5*/f32[16,12...) while((s32[]{:T(128)}, f32[128]{0:T(128)S(1)}, ...), condition=%wide.region_5.0_spmd, body=%wide.region_3.0_spmd.sunk | while | flops 393486 | bytes 138424 | solution.py:51
  209.9 5.6 all-to-all-start.1
  215.6 11.5 %all-to-all-done.1 = f32[32,16,128]{2,1,0:T(8,128)S(1)} async-done(((f32[32,16,128]{2,1,0:T(8,128)}), f32[32,16,128]{2,1,0:T(8,128)S(1)}, u32[]{:S(2)}, u32[]{:S(2)}) %all-to-all-start.1) | async-done | bytes 262176 | tf_op jit(solution)/shard_map/all_to_all | solution.py:92
  241.9 3.8 collective-permute-done.15
  256.2 3.5 collective-permute-start.18
  262.1 5.6 collective-permute-done.19
  274.7 3.8 collective-permute-done.21
  291.1 9.2 %all-to-all-start.2 = ((f32[32,16,128]{2,1,0:T(8,128)}), f32[32,16,128]{2,1,0:T(8,128)S(1)}, u32[]{:S(2)}, u32[]{:S(2)}) async-start(f32[32,16,128]{2,1,0:T(8,128)} %bitcast.39), calls=%async_computation.2 | async-start | bytes 524288 | tf_op jit(solution)/shard_map/all_to_all | solution.py:85
  300.3 11.7 %all-to-all-done.2 = f32[32,16,128]{2,1,0:T(8,128)S(1)} async-done(((f32[32,16,128]{2,1,0:T(8,128)}), f32[32,16,128]{2,1,0:T(8,128)S(1)}, u32[]{:S(2)}, u32[]{:S(2)}) %all-to-all-start.2) | async-done | bytes 262176 | tf_op jit(solution)/shard_map/all_to_all | solution.py:85
  312.0 12.7 %psum.22 = f32[16,128]{1,0:T(8,128)S(1)} all-reduce(f32[16,128]{1,0:T(8,128)S(1)} %reduce_sum.57), channel_id=1, replica_groups=mesh['fx'=32,'fy'=4,'fz'=2] {'fy','fz'}, use_global_device_ids=true, to_apply=%region_8.0 | all-reduce | flops 2048 | bytes 16384 | tf_op jit(solution)/shard_map/psum | solution.py:87
  324.9 98.6 %while.49 = (s32[]{:T(128)}, f32[128]{0:T(128)S(1)}, f32[16,128]{1,0:T(8,128)S(1)}, s32[16]{0:T(128)S(1)}, f32[16,128,128]{2,1,0:T(8,128)}, /*index=5*/f32[16,12...) while((s32[]{:T(128)}, f32[128]{0:T(128)S(1)}, ...), condition=%wide.region_11.0_spmd, body=%wide.region_9.0_spmd.sunk | while | flops 393486 | bytes 138424 | solution.py:51
  423.8 16.6 %all_to_all.42 = f32[32,16,128]{2,1,0:T(8,128)S(1)} all-to-all(f32[32,16,128]{2,1,0:T(8,128)S(1)} %stack.7), channel_id=1, replica_groups=mesh['fx'=32,'fy'=4,'fz'=2] {'fx'}, dimensions={0} | all-to-all | bytes 524288 | tf_op jit(solution)/shard_map/all_to_all | solution.py:92
  455.4 3.8 collective-permute-done.27
  469.6 3.5 collective-permute-start.30
  475.5 5.5 collective-permute-done.31
  488.7 3.8 collective-permute-done.33
  504.0 8.9 %all-to-all-start.4 = ((f32[32,16,128]{2,1,0:T(8,128)}), f32[32,16,128]{2,1,0:T(8,128)S(1)}, u32[]{:S(2)}, u32[]{:S(2)}) async-start(f32[32,16,128]{2,1,0:T(8,128)} %bitcast.44), calls=%async_computation.4 | async-start | bytes 524288 | tf_op jit(solution)/shard_map/all_to_all | solution.py:85
  512.9 11.7 %all-to-all-done.4 = f32[32,16,128]{2,1,0:T(8,128)S(1)} async-done(((f32[32,16,128]{2,1,0:T(8,128)}), f32[32,16,128]{2,1,0:T(8,128)S(1)}, u32[]{:S(2)}, u32[]{:S(2)}) %all-to-all-start.4) | async-done | bytes 262176 | tf_op jit(solution)/shard_map/all_to_all | solution.py:85
  524.7 12.7 %psum.23 = f32[16,128]{1,0:T(8,128)S(1)} all-reduce(f32[16,128]{1,0:T(8,128)S(1)} %reduce_sum.59), channel_id=1, replica_groups=mesh['fx'=32,'fy'=4,'fz'=2] {'fy','fz'}, use_global_device_ids=true, to_apply=%region_14.0 | all-reduce | flops 2048 | bytes 16384 | tf_op jit(solution)/shard_map/psum | solution.py:87
  537.5 95.3 %while.50 = (s32[]{:T(128)}, f32[128]{0:T(128)S(1)}, f32[16,128]{1,0:T(8,128)S(1)}, s32[16]{0:T(128)S(1)}, f32[16,128,128]{2,1,0:T(8,128)}, /*index=5*/f32[16,12...) while((s32[]{:T(128)}, f32[128]{0:T(128)S(1)}, ...), condition=%wide.region_17.0_spmd, body=%wide.region_15.0_spmd.sunk | while | flops 393486 | bytes 138424 | solution.py:51
  633.1 16.6 %all_to_all.43 = f32[32,16,128]{2,1,0:T(8,128)S(1)} all-to-all(f32[32,16,128]{2,1,0:T(8,128)S(1)} %stack.8), channel_id=1, replica_groups=mesh['fx'=32,'fy'=4,'fz'=2] {'fx'}, dimensions={0} | all-to-all | bytes 524288 | tf_op jit(solution)/shard_map/all_to_all | solution.py:92
  (446 shorter events, 334.8 us)
Async XLA Ops:
  2.2 5.9 collective-permute-start
  5.7 5.8 collective-permute-start.1
  14.6 5.1 collective-permute-start.2
  18.4 5.7 collective-permute-start.3
  27.1 4.4 collective-permute-start.4
  34.5 5.9 collective-permute-start.6
  37.7 7.5 %collective-permute-start.7 = (f32[5,8,1,128]{3,0,2,1:T(8,128)S(1)}, f32[5,8,1,128]{3,0,2,1:T(8,128)S(1)}, u32[]{:S(2)}, u32[]{:S(2)}) collective-permute-start(f32[5,8,1,128]{3,0,2,1:T(8,128)S(1)} %get-tuple-element.528), channel_id=1, source_target_pairs={{8,0},{16,8},{24,16},{32,24},{40,32},{48,40},{56,48},{64,56},{72,6... | collective-permute-start | bytes 61448 | tf_op jit(solution)/shard_map/ppermute | solution.py:21
  46.7 5.1 collective-permute-start.8
  50.5 5.8 collective-permute-start.9
  58.7 5.8 collective-permute-start.10
  60.0 5.2 collective-permute-start.11
  71.8 25.6 %all-to-all-start = ((f32[32,16,128]{2,1,0:T(8,128)}), f32[32,16,128]{2,1,0:T(8,128)S(1)}, u32[]{:S(2)}, u32[]{:S(2)}) async-start(f32[32,16,128]{2,1,0:T(8,128)} %bitcast.34), calls=%async_computation | async-start | bytes 524288 | tf_op jit(solution)/shard_map/all_to_all | solution.py:85
  209.9 17.2 %all-to-all-start.1 = ((f32[32,16,128]{2,1,0:T(8,128)}), f32[32,16,128]{2,1,0:T(8,128)S(1)}, u32[]{:S(2)}, u32[]{:S(2)}) async-start(f32[32,16,128]{2,1,0:T(8,128)} %stack.6), calls=%async_computation.1 | async-start | bytes 524288 | tf_op jit(solution)/shard_map/all_to_all | solution.py:92
  227.7 5.9 collective-permute-start.12
  231.0 5.8 collective-permute-start.13
  240.0 5.7 collective-permute-start.15
  248.7 4.4 collective-permute-start.16
  256.2 5.9 collective-permute-start.18
  259.7 7.9 %collective-permute-start.19 = (f32[5,8,1,128]{3,0,2,1:T(8,128)S(1)}, f32[5,8,1,128]{3,0,2,1:T(8,128)S(1)}, u32[]{:S(2)}, u32[]{:S(2)}) collective-permute-start(f32[5,8,1,128]{3,0,2,1:T(8,128)S(1)} %get-tuple-element.524), channel_id=1, source_target_pairs={{8,0},{16,8},{24,16},{32,24},{40,32},{48,40},{56,48},{64,56},{72,6... | collective-permute-start | bytes 61448 | tf_op jit(solution)/shard_map/ppermute | solution.py:21
  272.8 5.7 collective-permute-start.21
  281.5 4.4 collective-permute-start.22
  291.1 20.9 %all-to-all-start.2 = ((f32[32,16,128]{2,1,0:T(8,128)}), f32[32,16,128]{2,1,0:T(8,128)S(1)}, u32[]{:S(2)}, u32[]{:S(2)}) async-start(f32[32,16,128]{2,1,0:T(8,128)} %bitcast.39), calls=%async_computation.2 | async-start | bytes 524288 | tf_op jit(solution)/shard_map/all_to_all | solution.py:85
  440.9 6.1 collective-permute-start.24
  444.3 5.8 collective-permute-start.25
  453.5 5.7 collective-permute-start.27
  462.1 4.4 collective-permute-start.28
  463.4 4.2 collective-permute-start.29
  469.6 5.9 collective-permute-start.30
  473.1 7.9 %collective-permute-start.31 = (f32[5,8,1,128]{3,0,2,1:T(8,128)S(1)}, f32[5,8,1,128]{3,0,2,1:T(8,128)S(1)}, u32[]{:S(2)}, u32[]{:S(2)}) collective-permute-start(f32[5,8,1,128]{3,0,2,1:T(8,128)S(1)} %get-tuple-element.520), channel_id=1, source_target_pairs={{8,0},{16,8},{24,16},{32,24},{40,32},{48,40},{56,48},{64,56},{72,6... | collective-permute-start | bytes 61448 | tf_op jit(solution)/shard_map/ppermute | solution.py:21
  486.8 5.7 collective-permute-start.33
  495.5 4.4 collective-permute-start.34
  504.0 20.6 %all-to-all-start.4 = ((f32[32,16,128]{2,1,0:T(8,128)}), f32[32,16,128]{2,1,0:T(8,128)S(1)}, u32[]{:S(2)}, u32[]{:S(2)}) async-start(f32[32,16,128]{2,1,0:T(8,128)} %bitcast.44), calls=%async_computation.4 | async-start | bytes 524288 | tf_op jit(solution)/shard_map/all_to_all | solution.py:85
  (37 other events, 806.6 us)
